TPU v7x, 128 devices: a whole 4x4x4 slice. The times are simulated.
128 devices in a mesh: row: 16 (over x, y), col: 8 (over z, core).
Axes of the slice: x: 4, y: 4, z: 4, core: 2. Of those that a mesh axis runs over, the one named last changes fastest.
Arguments:
- orbitals: bfloat16 [131072, 512], P(('row', 'col')), may hold values from -6 to 6
- coulomb: bfloat16 [32768, 32768], P('row', 'col'), may hold values from -0.0014648438 to 0.0014648438
- interp: bfloat16 [131072, 1024], P(('row', 'col')), may hold values from -0.1875 to 0.1875
- box_counts: int32 [128], replicated, may hold values from 1 to 768, 32768 in all
- owner_map: int32 [32768], replicated, may hold values from 0 to 32767, as said below
- grid_rows: int32 [128, 1024], P(('row', 'col')), may hold values from 0 to 1023, each once within a row
- listed: int32 [128, 1024], P(('row', 'col')), may hold values from 0 to 255
Outputs:
- exchange_action: float32 [131072, 512], P(('row', 'col'))
Inputs may be any that keep to these rules, and one draw needn't show every extreme that they name: `box_counts`: the counts sum to 32768; the largest is exactly 768. `owner_map`: A permutation of the 32768 positions; a point's owner is position // 256. No box holds more than 6 points of one owner, and the box with 768 points holds exactly 6 of some owner. `grid_rows`: each row is a permutation.
All inputs are finite; a program needn't handle non-finite values.
Results may differ from a plain program's by a relative error of at most 0.012.
Values may be sent and summed in bfloat16 or wider, within the bound.
A program may use at most 128 MiB of HBM per device.

v0:
```python
import jax
import jax.numpy as jnp
from jax import lax
from jax.sharding import PartitionSpec as P

NORB = 512
LIST = 1024
OWN = 256
SLOTS = 768


def copy_for_each(x, axis):
    copies = jnp.broadcast_to(x, (lax.axis_size(axis), *x.shape))
    return lax.all_to_all(copies, axis, split_axis=0, concat_axis=0, tiled=True)


def in_order(parts, dim):
    parts = jnp.moveaxis(parts, 0, dim)
    dims = parts.shape
    return parts.reshape(*dims[:dim], dims[dim] * dims[dim + 1], *dims[dim + 2 :])


def gather_directly(x, axis, dim):
    parts = copy_for_each(x, axis)
    return in_order(parts, dim)


def add_block(shard_rows, left_rows, kernel_tile):
    pair_tile = jnp.einsum(
        "ak,bk->ab", left_rows, shard_rows, preferred_element_type=jnp.float32
    ).astype(jnp.bfloat16)
    weighted = (pair_tile.astype(jnp.float32) * kernel_tile.astype(jnp.float32)).astype(
        jnp.bfloat16
    )
    return jnp.dot(weighted, shard_rows, preferred_element_type=jnp.float32)


def shards(orbitals, coulomb, interp, box_counts, owner_map, grid_rows, listed):
    row_count = lax.axis_size("row")
    col_count = lax.axis_size("col")
    box_total = row_count * col_count
    point_total = OWN * box_total
    capacity = (SLOTS + box_total - 1) // box_total
    per_owner = LIST // box_total
    my_box = lax.axis_index("row") * col_count + lax.axis_index("col")
    box_ids = jnp.arange(box_total, dtype=jnp.int32)
    first_point = jnp.sum(jnp.where(box_ids < my_box, box_counts, 0))
    my_count = jnp.sum(jnp.where(box_ids == my_box, box_counts, 0))
    slot_ids = jnp.arange(SLOTS, dtype=jnp.int32)
    is_live = slot_ids < my_count
    listing = jnp.minimum(first_point + slot_ids, point_total - 1)
    owner_ids = owner_map[listing] // OWN
    matches = (
        (owner_ids[:, None] == owner_ids[None, :])
        & is_live[None, :]
        & (slot_ids[None, :] < slot_ids[:, None])
    )
    pair_rank = jnp.sum(matches.astype(jnp.int32), axis=1)
    target = jnp.where(is_live, owner_ids * capacity + pair_rank, box_total * capacity)
    dest_slots = jnp.arange(box_total * capacity, dtype=jnp.int32)
    hits = target[None, :] == dest_slots[:, None]
    source_slot = jnp.sum(jnp.where(hits, slot_ids[None, :], 0), axis=1)
    filled = jnp.any(hits, axis=1)
    picked = orbitals[grid_rows[0, source_slot]]
    outgoing = jnp.where(filled[:, None], picked, jnp.zeros_like(picked))
    received = lax.all_to_all(
        outgoing.reshape(box_total, capacity, NORB),
        ("row", "col"),
        split_axis=0,
        concat_axis=0,
        tiled=True,
    )
    received = received.reshape(box_total * capacity, NORB)
    wanted_pos = my_box * OWN + jnp.arange(OWN, dtype=jnp.int32)
    all_listing = jnp.arange(point_total, dtype=jnp.int32)
    my_points = jnp.sum(
        jnp.where(owner_map[None, :] == wanted_pos[:, None], all_listing[None, :], 0), axis=1
    )
    box_ends = jnp.cumsum(box_counts)
    source = jnp.sum((my_points[:, None] >= box_ends[None, :]).astype(jnp.int32), axis=1)
    earlier = (source[:, None] == source[None, :]) & (my_points[None, :] < my_points[:, None])
    source_rank = jnp.sum(earlier.astype(jnp.int32), axis=1)
    owned_rows = received[source * capacity + source_rank]
    left_rows = gather_directly(owned_rows, "col", 0)
    partial_sums = add_block(
        lax.all_gather(owned_rows, "row", axis=0, tiled=True), left_rows, coulomb
    )
    owned_result = lax.psum_scatter(partial_sums, "col", scatter_dimension=0, tiled=True).astype(
        jnp.bfloat16
    )
    wanted = listed[0].reshape(box_total, per_owner)
    fetched = lax.all_to_all(
        owned_result[
            lax.all_to_all(wanted, ("row", "col"), split_axis=0, concat_axis=0, tiled=True)
        ],
        ("row", "col"),
        split_axis=0,
        concat_axis=0,
        tiled=True,
    )
    chosen_rows = fetched.reshape(LIST, NORB)
    return -jnp.dot(interp, chosen_rows, preferred_element_type=jnp.float32)


def solution(mesh):
    return jax.shard_map(
        shards,
        mesh=mesh,
        in_specs=(
            P(("row", "col"), None),
            P("row", "col"),
            P(("row", "col"), None),
            P(),
            P(),
            P(("row", "col"), None),
            P(("row", "col"), None),
        ),
        out_specs=P(("row", "col"), None),
        check_vma=False,
    )
```

profile of v0, /device:TPU:1, one launch (start us, length us, event | category | flops | bytes accessed | tf_op | source)
XLA Modules:
  0.0 216.9 jit_solution(2038270782259860773)
XLA Ops:
  6.5 0.0 copy-start
  6.5 0.0 copy-start.1
  6.5 1.5 fusion.12
  8.1 0.7 fusion.7
  8.8 4.7 %gather_fusion = s32[768]{0:T(1024)S(1)} fusion(s32[32768]{0:T(1024)} %param.11, s32[1024]{0:T(1024)S(1)} %pad_clamp_fusion.2), kind=kCustom, calls=%fused_computation | custom fusion | bytes 9216 | tf_op jit(solution)/shard_map/gather | solution.py:52
  13.5 0.0 copy-start.3
  13.5 0.7 iota_compare_fusion.2
  14.2 0.4 convert_reduce_fusion
  14.7 0.7 add_select_fusion.1
  15.3 0.3 select_reduce_fusion.1
  15.6 0.3 fusion.2
  16.0 0.0 copy-done.1
  16.0 4.7 %gather_fusion.1 = s32[768]{0:T(1024)S(1)} fusion(s32[1,1024]{1,0:T(1,128)S(1)} %copy-done.1, s32[768]{0:T(1024)S(1)} %fusion.11), kind=kCustom, calls=%fused_computation.1 | custom fusion | bytes 12288 | tf_op jit(solution)/shard_map/gather | solution.py:64
  20.7 0.0 copy-done.3
  20.7 3.3 %gather_fusion.2 = bf16[768,512]{1,0:T(8,128)(2,1)} fusion(bf16[1024,512]{1,0:T(8,128)(2,1)S(1)} %copy-done.3, s32[1024]{0:T(1024)S(1)} %pad_clamp_fusion.1), kind=kCustom, calls=%fused_computation.2 | custom fusion | bytes 1575936 | tf_op jit(solution)/shard_map/gather | solution.py:64
  24.1 1.3 gather.23
  25.4 0.0 copy-start.2
  25.4 0.0 copy-start.5
  25.4 0.2 broadcast_in_dim.47
  25.6 1.2 broadcast_select_fusion
  26.8 12.0 %all-to-all-start = ((bf16[128,6,512]{2,1,0:T(8,128)(2,1)}), bf16[128,6,512]{2,1,0:T(8,128)(2,1)}, u32[]{:S(2)}, u32[]{:S(2)}) async-start(bf16[128,6,512]{2,1,0:T(8,128)(2,1)} %broadcast_select_fusion), calls=%async_computation | async-start | bytes 2097152 | tf_op jit(solution)/shard_map/all_to_all | solution.py:66
  38.7 0.0 all-gather.3.cloned.1.call-start
  38.8 0.0 copy-done.2
  38.8 4.6 %select_reduce_fusion = s32[256]{0:T(256)S(1)} fusion(s32[32768]{0:T(1024)S(1)} %copy-done.2, s32[256]{0:T(256)S(1)} %iota_add_fusion), kind=kLoop, calls=%fused_computation.6 | loop fusion | flops 25165568 | bytes 133120 | tf_op jit(solution)/shard_map/reduce_sum | solution.py:76
  43.4 0.0 copy-done.5
  43.4 0.1 copy.15
  43.5 0.2 reduce-window.8
  43.7 0.1 reduce.3
  43.8 0.2 convert_reduce_fusion.2
  44.0 0.2 convert_reduce_fusion.1
  44.3 13.4 %all-to-all-done = bf16[128,6,512]{2,1,0:T(8,128)(2,1)} async-done(((bf16[128,6,512]{2,1,0:T(8,128)(2,1)}), bf16[128,6,512]{2,1,0:T(8,128)(2,1)}, u32[]{:S(2)}, u32[]{:S(2)}) %all-to-all-start) | async-done | bytes 786464 | tf_op jit(solution)/shard_map/all_to_all | solution.py:66
  57.7 1.4 reshape.199
  59.0 1.9 gather_fusion.3
  60.9 0.0 all-gather.3.cloned.1.call-update
  60.9 0.0 reduce-scatter.2.cloned.1.call-start
  61.0 1.1 broadcast_in_dim.79
  62.1 30.8 %all_to_all.27 = bf16[8,256,512]{2,1,0:T(8,128)(2,1)} all-to-all(bf16[8,256,512]{2,1,0:T(8,128)(2,1)S(1)} %broadcast_in_dim.79), channel_id=1, replica_groups=mesh['row'=16,'col'=8] {'col'}, dimensions={0} | all-to-all | bytes 4194304 | tf_op jit(solution)/shard_map/all_to_all | solution.py:14
  92.9 15.8 %all-gather.3.cloned.1.call-done = bf16[4096,512]{1,0:T(8,128)(2,1)} async-done(((bf16[256,512]{1,0:T(8,128)(2,1)}), bf16[4096,512]{1,0:T(8,128)(2,1)}) %all-gather.3.cloned.1.call-update) | async-done | bytes 4194320 | tf_op jit(solution)/shard_map/all_gather | solution.py:86
  108.7 26.1 %fusion = f32[2048,512]{1,0:T(8,128)} fusion(bf16[4096,512]{1,0:T(8,128)(2,1)} %all-gather.3.cloned.1.call-done, bf16[2048,4096]{1,0:T(8,128)(2,1)} %param.8, bf16[2048,512]{1,0:T(8,128)(2,1)} %bitcast.27), kind=kOutput, calls=%fused_computation.7 | convolution fusion | flops 17213423616 | bytes 27262976 | tf_op jit(solution)/shard_map/dot_general | solution.py:35
  134.8 0.0 copy-start.4
  134.8 0.0 reduce-scatter.2.cloned.1.call-update
  134.8 0.5 broadcast.260
  135.3 0.1 copy-done.4
  135.5 0.7 reduce.10
  136.1 0.1 all_to_all.19
  136.2 17.2 %all_to_all.28 = s32[128,1,8]{2,1,0:T(1,128)S(1)} all-to-all(s32[128,1,8]{2,1,0:T(1,128)S(1)} %bitcast.28), channel_id=1, replica_groups=mesh['row'=16,'col'=8] {'row','col'}, dimensions={0} | all-to-all | bytes 8192 | tf_op jit(solution)/shard_map/all_to_all | solution.py:94
  153.4 0.1 reshape.236
  153.5 16.8 %reduce-scatter.2.cloned.1.call-done = f32[256,512]{1,0:T(8,128)} async-done(((f32[2048,512]{1,0:T(8,128)}), f32[256,512]{1,0:T(8,128)}) %reduce-scatter.2.cloned.1.call-update) | async-done | bytes 524304 | tf_op jit(solution)/shard_map/reduce_scatter | solution.py:88
  170.3 1.1 convert_element_type.31
  171.4 4.0 %gather_fusion.4 = bf16[1024,512]{1,0:T(8,128)(2,1)S(1)} fusion(bf16[256,512]{1,0:T(8,128)(2,1)S(1)} %convert_element_type.31, s32[1024]{0:T(1024)S(1)} %broadcast_clamp_fusion), kind=kCustom, calls=%fused_computation.4 | custom fusion | bytes 2101248 | tf_op jit(solution)/shard_map/gather | solution.py:93
  175.4 29.2 %all_to_all.29 = bf16[128,8,512]{2,1,0:T(8,128)(2,1)S(1)} all-to-all(bf16[128,8,512]{2,1,0:T(8,128)(2,1)S(1)} %bitcast.26), channel_id=1, replica_groups=mesh['row'=16,'col'=8] {'row','col'}, dimensions={0} | all-to-all | bytes 2097152 | tf_op jit(solution)/shard_map/all_to_all | solution.py:92
  204.5 0.0 copy-done
  204.5 2.6 %negate_bitcast_fusion = f32[1024,512]{0,1:T(8,128)} fusion(bf16[1024,1024]{1,0:T(8,128)(2,1)S(1)} %copy-done, bf16[128,8,512]{2,1,0:T(8,128)(2,1)S(1)} %all_to_all.29), kind=kOutput, calls=%fused_computation.15 | convolution fusion | flops 1074266112 | bytes 5242880 | tf_op jit(solution)/shard_map/dot_general | solution.py:102
  207.2 2.9 %copy.17 = f32[1024,512]{1,0:T(8,128)} copy(f32[1024,512]{0,1:T(8,128)} %negate_bitcast_fusion) | data formatting | bytes 4194304 | tf_op jit(solution)/shard_map/neg | solution.py:102
  (11 shorter events, 0.1 us)
Async XLA Ops:
  6.5 198.0 %copy-start = (bf16[1024,1024]{1,0:T(8,128)(2,1)S(1)}, bf16[1024,1024]{1,0:T(8,128)(2,1)}, u32[]{:S(2)}) copy-start(bf16[1024,1024]{1,0:T(8,128)(2,1)} %param.9) | copy-start | bytes 6291460
  6.5 9.5 %copy-start.1 = (s32[1,1024]{1,0:T(1,128)S(1)}, s32[1,1024]{1,0:T(1,128)}, u32[]{:S(2)}) copy-start(s32[1,1024]{1,0:T(1,128)} %param.12) | copy-start | bytes 12292
  13.5 7.3 %copy-start.3 = (bf16[1024,512]{1,0:T(8,128)(2,1)S(1)}, bf16[1024,512]{1,0:T(8,128)(2,1)}, u32[]{:S(2)}) copy-start(bf16[1024,512]{1,0:T(8,128)(2,1)} %param.7) | copy-start | bytes 3145732
  25.4 13.4 %copy-start.2 = (s32[32768]{0:T(1024)S(1)}, s32[32768]{0:T(1024)}, u32[]{:S(2)}) copy-start(s32[32768]{0:T(1024)} %param.11) | copy-start | bytes 393220
  25.4 18.0 %copy-start.5 = (s32[128]{0:T(128)S(1)}, s32[128]{0:T(128)}, u32[]{:S(2)}) copy-start(s32[128]{0:T(128)} %param.10) | copy-start | bytes 1540
  26.8 30.9 %all-to-all-start = ((bf16[128,6,512]{2,1,0:T(8,128)(2,1)}), bf16[128,6,512]{2,1,0:T(8,128)(2,1)}, u32[]{:S(2)}, u32[]{:S(2)}) async-start(bf16[128,6,512]{2,1,0:T(8,128)(2,1)} %broadcast_select_fusion), calls=%async_computation | async-start | bytes 2097152 | tf_op jit(solution)/shard_map/all_to_all | solution.py:66
  38.7 70.0 %all-gather.3.cloned.1.call-start = ((), (), s32[]{:S(2)}) async-start(), calls=%async_computation.6 | async-start | bytes 4456448 | tf_op jit(solution)/shard_map/all_gather | solution.py:86
  60.9 109.4 %reduce-scatter.2.cloned.1.call-start = ((), (), s32[]{:S(2)}) async-start(), calls=%async_computation.5 | async-start | bytes 4718592 | tf_op jit(solution)/shard_map/reduce_scatter | solution.py:88
  134.8 0.7 copy-start.4
Sparse Core Ops, SparseCore 0:
  61.0 47.5 all-gather.2
  134.9 35.3 reduce-scatter.1
where the time goes:
time: 217 us
  blocking collectives  77.1 us (36%)
  waiting for transfers between devices  46 us (21%)
  matrix products  28.8 us (13%)
  local copies, waits for them, and re-layouts  26.3 us (12%)
  between operations  13.7 us (6%)
  other arithmetic  13 us (6%)
  starting transfers between devices  12 us (6%)
    all_to_all x1, blocking collectives, copy_for_each(): return lax.all_to_all(copies, axis, split_axis=0, concat_axis=0, tiled=True)  30.8 us
    all_to_all x1, blocking collectives, shards(): lax.all_to_all(owned_result[lax.all_to_all(wanted, ('row', 'col'), split_...  29.2 us
    dot_general x1, matrix products, add_block(): return jnp.dot(weighted, shard_rows, preferred_element_type=jnp.float32)  26.1 us
    all_to_all x1, blocking collectives, shards(): lax.all_to_all(wanted, ('row', 'col'), split_axis=0, concat_axis=0, tiled...  17.2 us
    reduce_scatter x1, waiting for transfers between devices, shards(): lax.psum_scatter(partial_sums, 'col', scatter_dimension=0, tiled=True)  16.8 us
    all_gather x1, waiting for transfers between devices, shards(): lax.all_gather(owned_rows, 'row', axis=0, tiled=True)  15.8 us
    all_to_all x1, waiting for transfers between devices, shards(): lax.all_to_all(outgoing.reshape(box_total, capacity, NORB), ('row', 'col'...  13.4 us
    all_to_all x1, starting transfers between devices, shards(): lax.all_to_all(outgoing.reshape(box_total, capacity, NORB), ('row', 'col'...  12 us
  transfers between devices with their start and end apart: 3, of which 3 were waited for; matrix products, arithmetic and copies ran while one was open for 4% of the time, Pallas kernels for 0%

commit v1 on v0

--- a/solution.py
+++ b/solution.py
@@ -1,3 +1,4 @@
+import functools
 import jax
 import jax.numpy as jnp
 from jax import lax
@@ -7,6 +8,19 @@
 LIST = 1024
 OWN = 256
 SLOTS = 768
+
+
+def spots_scan(local_values, net_axis, dim_k):
+    pages = []
+    for _ in range(lax.axis_size(net_axis)):
+        pages.append(local_values)
+    y2 = jnp.concatenate(
+        lax.all_to_all(jnp.stack(pages, 0), axis_name=net_axis, split_axis=0, concat_axis=0), dim_k
+    )
+    return y2
+
+
+convert_results = functools.partial(spots_scan, net_axis="row", dim_k=0)
 
 
 def copy_for_each(x, axis):
@@ -82,9 +96,7 @@
     source_rank = jnp.sum(earlier.astype(jnp.int32), axis=1)
     owned_rows = received[source * capacity + source_rank]
     left_rows = gather_directly(owned_rows, "col", 0)
-    partial_sums = add_block(
-        lax.all_gather(owned_rows, "row", axis=0, tiled=True), left_rows, coulomb
-    )
+    partial_sums = add_block(convert_results(owned_rows), left_rows, coulomb)
     owned_result = lax.psum_scatter(partial_sums, "col", scatter_dimension=0, tiled=True).astype(
         jnp.bfloat16
     )

time: 217 us -> 252 us (1.16)
  blocking collectives: 77.1 us -> 129 us
  waiting for transfers between devices: 46 us -> 30.2 us
    all_to_all x0 -> x1, blocking collectives: none -> 52.4 us  [spots_scan(): lax.all_to_all(jnp.stack(pages, 0), axis_name=net_axis, split_axis=0, con...]
    all_gather x1 -> x0, waiting for transfers between devices: 15.8 us -> none  [shards(): lax.all_gather(owned_rows, 'row', axis=0, tiled=True)]
  transfers between devices with their start and end apart: 3 -> 2, of which waited for: 3 -> 2; matrix products, arithmetic and copies ran while one was open for 4% -> 3% of each run, Pallas kernels for 0% -> 0%
where the time goes in v1:
time: 252 us; the launch traced here: 251 us
  blocking collectives  129 us (51%)
  waiting for transfers between devices  30.2 us (12%)
  matrix products  28.8 us (11%)
  local copies, waits for them, and re-layouts  25.1 us (10%)
  between operations  13.7 us (5%)
  other arithmetic  13 us (5%)
  starting transfers between devices  12 us (5%)
    all_to_all x1, blocking collectives, spots_scan(): lax.all_to_all(jnp.stack(pages, 0), axis_name=net_axis, split_axis=0, con...  52.4 us
    all_to_all x1, blocking collectives, copy_for_each(): return lax.all_to_all(copies, axis, split_axis=0, concat_axis=0, tiled=True)  30.8 us
    all_to_all x1, blocking collectives, shards(): lax.all_to_all(owned_result[lax.all_to_all(wanted, ('row', 'col'), split_...  29.3 us
    dot_general x1, matrix products, add_block(): return jnp.dot(weighted, shard_rows, preferred_element_type=jnp.float32)  26.1 us
    reduce_scatter x1, waiting for transfers between devices, shards(): lax.psum_scatter(partial_sums, 'col', scatter_dimension=0, tiled=True)  16.8 us
    all_to_all x1, blocking collectives, shards(): lax.all_to_all(wanted, ('row', 'col'), split_axis=0, concat_axis=0, tiled...  16 us
    all_to_all x1, waiting for transfers between devices, shards(): lax.all_to_all(outgoing.reshape(box_total, capacity, NORB), ('row', 'col'...  13.4 us
    all_to_all x1, starting transfers between devices, shards(): lax.all_to_all(outgoing.reshape(box_total, capacity, NORB), ('row', 'col'...  12 us
  transfers between devices with their start and end apart: 2, of which 2 were waited for; matrix products, arithmetic and copies ran while one was open for 3% of the time, Pallas kernels for 0%

profile of v1, /device:TPU:1, one launch (start us, length us, event | category | flops | bytes accessed | tf_op | source)
XLA Modules:
  0.0 251.2 jit_solution(15834934665047214651)
XLA Ops:
  6.5 0.0 copy-start
  6.5 0.0 copy-start.1
  6.5 1.5 fusion.12
  8.1 0.7 fusion.7
  8.8 4.7 %gather_fusion = s32[768]{0:T(1024)S(1)} fusion(s32[32768]{0:T(1024)} %param.11, s32[1024]{0:T(1024)S(1)} %pad_clamp_fusion.2), kind=kCustom, calls=%fused_computation | custom fusion | bytes 9216 | tf_op jit(solution)/shard_map/gather | solution.py:66
  13.5 0.0 copy-start.3
  13.5 0.7 iota_compare_fusion.2
  14.2 0.4 convert_reduce_fusion
  14.7 0.7 add_select_fusion.1
  15.3 0.3 select_reduce_fusion.1
  15.6 0.3 fusion.2
  16.0 0.0 copy-done.1
  16.0 4.7 %gather_fusion.1 = s32[768]{0:T(1024)S(1)} fusion(s32[1,1024]{1,0:T(1,128)S(1)} %copy-done.1, s32[768]{0:T(1024)S(1)} %fusion.11), kind=kCustom, calls=%fused_computation.1 | custom fusion | bytes 12288 | tf_op jit(solution)/shard_map/gather | solution.py:78
  20.7 0.0 copy-done.3
  20.7 3.3 %gather_fusion.2 = bf16[768,512]{1,0:T(8,128)(2,1)} fusion(bf16[1024,512]{1,0:T(8,128)(2,1)S(1)} %copy-done.3, s32[1024]{0:T(1024)S(1)} %pad_clamp_fusion.1), kind=kCustom, calls=%fused_computation.2 | custom fusion | bytes 1575936 | tf_op jit(solution)/shard_map/gather | solution.py:78
  24.1 1.3 gather.23
  25.4 0.0 copy-start.2
  25.4 0.0 copy-start.5
  25.4 0.2 broadcast_in_dim.47
  25.6 1.2 broadcast_select_fusion
  26.8 12.0 %all-to-all-start = ((bf16[128,6,512]{2,1,0:T(8,128)(2,1)}), bf16[128,6,512]{2,1,0:T(8,128)(2,1)}, u32[]{:S(2)}, u32[]{:S(2)}) async-start(bf16[128,6,512]{2,1,0:T(8,128)(2,1)} %broadcast_select_fusion), calls=%async_computation | async-start | bytes 2097152 | tf_op jit(solution)/shard_map/all_to_all | solution.py:80
  38.7 0.0 reduce-scatter.2.cloned.1.call-start
  38.8 0.0 copy-done.2
  38.8 4.6 %select_reduce_fusion = s32[256]{0:T(256)S(1)} fusion(s32[32768]{0:T(1024)S(1)} %copy-done.2, s32[256]{0:T(256)S(1)} %iota_add_fusion), kind=kLoop, calls=%fused_computation.6 | loop fusion | flops 25165568 | bytes 133120 | tf_op jit(solution)/shard_map/reduce_sum | solution.py:90
  43.4 0.0 copy-done.5
  43.4 0.1 copy.15
  43.5 0.2 reduce-window.8
  43.7 0.1 reduce.3
  43.8 0.2 convert_reduce_fusion.2
  44.0 0.2 convert_reduce_fusion.1
  44.3 13.4 %all-to-all-done = bf16[128,6,512]{2,1,0:T(8,128)(2,1)} async-done(((bf16[128,6,512]{2,1,0:T(8,128)(2,1)}), bf16[128,6,512]{2,1,0:T(8,128)(2,1)}, u32[]{:S(2)}, u32[]{:S(2)}) %all-to-all-start) | async-done | bytes 786464 | tf_op jit(solution)/shard_map/all_to_all | solution.py:80
  57.7 1.4 reshape.204
  59.0 1.2 gather_fusion.3
  60.2 0.2 broadcast_in_dim.79
  60.4 30.8 %all_to_all.32 = bf16[8,256,512]{2,1,0:T(8,128)(2,1)} all-to-all(bf16[8,256,512]{2,1,0:T(8,128)(2,1)S(1)} %broadcast_in_dim.79), channel_id=1, replica_groups=mesh['row'=16,'col'=8] {'col'}, dimensions={0} | all-to-all | bytes 4194304 | tf_op jit(solution)/shard_map/all_to_all | solution.py:28
  91.2 0.4 stack.2
  91.6 52.4 %all_to_all.33 = bf16[16,256,512]{2,1,0:T(8,128)(2,1)} all-to-all(bf16[16,256,512]{2,1,0:T(8,128)(2,1)S(1)} %stack.2), channel_id=1, replica_groups=mesh['row'=16,'col'=8] {'row'}, dimensions={0} | all-to-all | bytes 8388608 | tf_op jit(solution)/shard_map/all_to_all | solution.py:18
  144.0 26.1 %fusion = f32[2048,512]{1,0:T(8,128)} fusion(bf16[4096,512]{1,0:T(8,128)(2,1)} %bitcast.28, bf16[2048,4096]{1,0:T(8,128)(2,1)} %param.8, bf16[2048,512]{1,0:T(8,128)(2,1)} %bitcast.29), kind=kOutput, calls=%fused_computation.7 | convolution fusion | flops 17213423616 | bytes 27262976 | tf_op jit(solution)/shard_map/dot_general | solution.py:49
  170.1 0.0 copy-start.4
  170.1 0.0 reduce-scatter.2.cloned.1.call-update
  170.1 0.5 broadcast.262
  170.7 0.1 copy-done.4
  170.8 0.7 reduce.10
  171.5 0.1 all_to_all.23
  171.6 16.0 %all_to_all.34 = s32[128,1,8]{2,1,0:T(1,128)S(1)} all-to-all(s32[128,1,8]{2,1,0:T(1,128)S(1)} %bitcast.30), channel_id=1, replica_groups=mesh['row'=16,'col'=8] {'row','col'}, dimensions={0} | all-to-all | bytes 8192 | tf_op jit(solution)/shard_map/all_to_all | solution.py:106
  187.6 0.1 reshape.242
  187.7 16.8 %reduce-scatter.2.cloned.1.call-done = f32[256,512]{1,0:T(8,128)} async-done(((f32[2048,512]{1,0:T(8,128)}), f32[256,512]{1,0:T(8,128)}) %reduce-scatter.2.cloned.1.call-update) | async-done | bytes 524304 | tf_op jit(solution)/shard_map/reduce_scatter | solution.py:100
  204.5 1.1 convert_element_type.31
  205.6 4.0 %gather_fusion.4 = bf16[1024,512]{1,0:T(8,128)(2,1)S(1)} fusion(bf16[256,512]{1,0:T(8,128)(2,1)S(1)} %convert_element_type.31, s32[1024]{0:T(1024)S(1)} %broadcast_clamp_fusion), kind=kCustom, calls=%fused_computation.4 | custom fusion | bytes 2101248 | tf_op jit(solution)/shard_map/gather | solution.py:105
  209.6 29.3 %all_to_all.35 = bf16[128,8,512]{2,1,0:T(8,128)(2,1)S(1)} all-to-all(bf16[128,8,512]{2,1,0:T(8,128)(2,1)S(1)} %bitcast.27), channel_id=1, replica_groups=mesh['row'=16,'col'=8] {'row','col'}, dimensions={0} | all-to-all | bytes 2097152 | tf_op jit(solution)/shard_map/all_to_all | solution.py:104
  238.9 0.0 copy-done
  238.9 2.7 %negate_bitcast_fusion = f32[1024,512]{0,1:T(8,128)} fusion(bf16[1024,1024]{1,0:T(8,128)(2,1)S(1)} %copy-done, bf16[128,8,512]{2,1,0:T(8,128)(2,1)S(1)} %all_to_all.35), kind=kOutput, calls=%fused_computation.15 | convolution fusion | flops 1074266112 | bytes 5242880 | tf_op jit(solution)/shard_map/dot_general | solution.py:114
  241.5 2.9 %copy.17 = f32[1024,512]{1,0:T(8,128)} copy(f32[1024,512]{0,1:T(8,128)} %negate_bitcast_fusion) | data formatting | bytes 4194304 | tf_op jit(solution)/shard_map/neg | solution.py:114
  (11 shorter events, 0.1 us)
Async XLA Ops:
  6.5 232.3 %copy-start = (bf16[1024,1024]{1,0:T(8,128)(2,1)S(1)}, bf16[1024,1024]{1,0:T(8,128)(2,1)}, u32[]{:S(2)}) copy-start(bf16[1024,1024]{1,0:T(8,128)(2,1)} %param.9) | copy-start | bytes 6291460
  6.5 9.5 %copy-start.1 = (s32[1,1024]{1,0:T(1,128)S(1)}, s32[1,1024]{1,0:T(1,128)}, u32[]{:S(2)}) copy-start(s32[1,1024]{1,0:T(1,128)} %param.12) | copy-start | bytes 12292
  13.5 7.3 %copy-start.3 = (bf16[1024,512]{1,0:T(8,128)(2,1)S(1)}, bf16[1024,512]{1,0:T(8,128)(2,1)}, u32[]{:S(2)}) copy-start(bf16[1024,512]{1,0:T(8,128)(2,1)} %param.7) | copy-start | bytes 3145732
  25.4 13.4 %copy-start.2 = (s32[32768]{0:T(1024)S(1)}, s32[32768]{0:T(1024)}, u32[]{:S(2)}) copy-start(s32[32768]{0:T(1024)} %param.11) | copy-start | bytes 393220
  25.4 18.0 %copy-start.5 = (s32[128]{0:T(128)S(1)}, s32[128]{0:T(128)}, u32[]{:S(2)}) copy-start(s32[128]{0:T(128)} %param.10) | copy-start | bytes 1540
  26.8 30.9 %all-to-all-start = ((bf16[128,6,512]{2,1,0:T(8,128)(2,1)}), bf16[128,6,512]{2,1,0:T(8,128)(2,1)}, u32[]{:S(2)}, u32[]{:S(2)}) async-start(bf16[128,6,512]{2,1,0:T(8,128)(2,1)} %broadcast_select_fusion), calls=%async_computation | async-start | bytes 2097152 | tf_op jit(solution)/shard_map/all_to_all | solution.py:80
  38.7 165.8 %reduce-scatter.2.cloned.1.call-start = ((), (), s32[]{:S(2)}) async-start(), calls=%async_computation.6 | async-start | bytes 4718592 | tf_op jit(solution)/shard_map/reduce_scatter | solution.py:100
  170.1 0.7 copy-start.4
Sparse Core Ops, SparseCore 0:
  170.3 34.2 reduce-scatter.1
